TPU v7x, 512 devices: a whole 4x4x16 slice. The times are simulated.
512 devices in a mesh: pipe: 32 (over y, z_lo, core), dp: 16 (over x, z_hi).
Axes of the slice: x: 4, y: 4, z: 16 (z_hi: 4, z_lo: 4; z = z_hi * 4 + z_lo), core: 2. Of those that a mesh axis runs over, the one named last changes fastest.
Arguments:
- section_inputs: bfloat16 [32, 2, 1024, 4096], P('pipe', None, 'dp'), may hold values from -6 to 6
- arriving: bfloat16 [32, 1024, 4096], P('pipe', 'dp'), may hold values from -2.5 to 2.5
- top_grads: bfloat16 [1, 1024, 4096], P(None, 'dp', 'pipe'), may hold values from -2.5 to 2.5
- project_weights: bfloat16 [32, 4096, 384], P('pipe', 'dp'), may hold values from -0.09375 to 0.09375
- output_weights: bfloat16 [32, 4096, 128], P('pipe', 'dp'), may hold values from -0.5 to 0.5
Outputs:
- project_grads: float32 [32, 4096, 384], P('pipe', 'dp')
- output_grads: float32 [32, 4096, 128], P('pipe', 'dp')
- passed_back: bfloat16 [32, 1024, 4096], P('pipe', 'dp')
All inputs are finite; a program needn't handle non-finite values.
Results may differ from a plain program's by a relative error of at most 0.015.
Values may be sent and summed in bfloat16 or wider, within the bound.
A program may use at most 64 MiB of HBM per device.

v0:
```python
import math

import jax
import jax.numpy as jnp
from jax import lax
from jax.sharding import Mesh
from jax.sharding import PartitionSpec as P

DP = ("dp_0", "dp_1")


EPSILON = 1e-06
CONTRACT_FIRST = (((0,), (0,)), ((), ()))
CONTRACT_LAST = (((1,), (1,)), ((), ()))


def side_by_side(arrays, axis, dim, along):
    both = jnp.concatenate(arrays, axis=along)
    out, at, finished = (lax.all_gather(both, axis, axis=dim, tiled=True), 0, [])
    for a in arrays:
        finished.append(lax.slice_in_dim(out, at, at + a.shape[along], axis=along))
        at += a.shape[along]
    return tuple(finished)


def in_order(pieces, dim):
    pieces = jnp.moveaxis(pieces, 0, dim)
    dims = pieces.shape
    return pieces.reshape(*dims[:dim], dims[dim] * dims[dim + 1], *dims[dim + 2 :])


def copy_for_each(value, axis):
    copies = jnp.broadcast_to(value, (lax.axis_size(axis), *value.shape))
    return lax.all_to_all(copies, axis, split_axis=0, concat_axis=0, tiled=True)


def gathered_copies(value, axis, dim):
    return in_order(copy_for_each(value, axis), dim)


def passed_along(value, axis, steps):
    count = lax.axis_size(axis)
    leading, last = (max(0, -steps), min(count, count - steps))
    return lax.ppermute(value, axis, [(source, source + steps) for source in range(leading, last)])


def summed_rows(value, axes, dim):
    for axis in axes:
        value = lax.psum_scatter(value, axis, scatter_dimension=dim, tiled=True)
    return value


def normalize(values):
    centered = values - jnp.mean(values, axis=-1, keepdims=True)
    inverse = lax.rsqrt(jnp.mean(centered * centered, axis=-1, keepdims=True) + EPSILON)
    return (centered * inverse, inverse)


def norm_back(gradient, normed, inverse):
    centered = gradient - jnp.mean(gradient, axis=-1, keepdims=True)
    return inverse * (centered - normed * jnp.mean(gradient * normed, axis=-1, keepdims=True))


def shards(section_inputs, arriving, top_grads, project_weights, output_weights):
    tick_count = section_inputs.shape[1]
    seq_len = section_inputs.shape[2]
    width = section_inputs.shape[3]
    head_size = output_weights.shape[2]
    root_size = math.sqrt(head_size)
    total_rows = tick_count * seq_len
    normed, inverse = normalize(section_inputs[0].reshape(total_rows, width).astype(jnp.float32))
    hidden = normed.astype(jnp.bfloat16)
    full_project, full_output = side_by_side((project_weights[0], output_weights[0]), DP, 0, 1)
    projected = jnp.dot(hidden, full_project, preferred_element_type=jnp.float32)
    query, query_scale = normalize(projected[:, :head_size])
    key_normed, key_scale = normalize(projected[:, head_size : 2 * head_size])
    query_half = query.astype(jnp.bfloat16).reshape(tick_count, seq_len, head_size)
    key_half = key_normed.astype(jnp.bfloat16).reshape(tick_count, seq_len, head_size)
    value_half = (
        projected[:, 2 * head_size :].astype(jnp.bfloat16).reshape(tick_count, seq_len, head_size)
    )
    scores = (
        jnp.einsum("ksh,kth->kst", query_half, key_half, preferred_element_type=jnp.float32)
        / root_size
    )
    powered = jnp.exp(scores)
    attention = powered / jnp.sum(powered, axis=-1, keepdims=True)
    attention_half = attention.astype(jnp.bfloat16)
    mixed_half = jnp.einsum(
        "kst,kth->ksh", attention_half, value_half, preferred_element_type=jnp.float32
    ).astype(jnp.bfloat16)
    later_grads = gathered_copies(top_grads, "pipe", 2)
    last_section = lax.axis_index("pipe") == lax.axis_size("pipe") - 1
    incoming = arriving[0]
    received = incoming
    passed = incoming
    sum_project = jnp.zeros((width, 3 * head_size), jnp.float32)
    sum_output = jnp.zeros((width, head_size), jnp.float32)
    for tick_index in range(tick_count):
        if tick_index > 0:
            incoming = jnp.where(last_section, later_grads[tick_index - 1], received)
        lower = tick_index * seq_len
        upper = lower + seq_len
        head_grad = jnp.dot(incoming, full_output, preferred_element_type=jnp.float32).astype(
            jnp.bfloat16
        )
        prob_grad = lax.dot_general(
            head_grad, value_half[tick_index], CONTRACT_LAST, preferred_element_type=jnp.float32
        )
        value_grad = lax.dot_general(
            attention_half[tick_index],
            head_grad,
            CONTRACT_FIRST,
            preferred_element_type=jnp.float32,
        ).astype(jnp.bfloat16)
        weighted = attention[tick_index]
        score_grad = (
            weighted
            * (prob_grad - jnp.sum(weighted * prob_grad, axis=-1, keepdims=True))
            / root_size
        ).astype(jnp.bfloat16)
        query_grad = jnp.dot(score_grad, key_half[tick_index], preferred_element_type=jnp.float32)
        key_grad = lax.dot_general(
            score_grad, query_half[tick_index], CONTRACT_FIRST, preferred_element_type=jnp.float32
        )
        normed_grads = jnp.concatenate(
            [
                norm_back(query_grad, query[lower:upper], query_scale[lower:upper]),
                norm_back(key_grad, key_normed[lower:upper], key_scale[lower:upper]),
            ],
            axis=1,
        ).astype(jnp.bfloat16)
        proj_grad = jnp.concatenate([normed_grads, value_grad], axis=1)
        hidden_grad = lax.dot_general(
            proj_grad, full_project, CONTRACT_LAST, preferred_element_type=jnp.float32
        )
        passed = (
            incoming.astype(jnp.float32)
            + norm_back(hidden_grad, normed[lower:upper], inverse[lower:upper])
        ).astype(jnp.bfloat16)
        if tick_index + 1 < tick_count:
            received = passed_along(passed, "pipe", -1)
        sum_project = sum_project + lax.dot_general(
            hidden[lower:upper], proj_grad, CONTRACT_FIRST, preferred_element_type=jnp.float32
        )
        sum_output = sum_output + lax.dot_general(
            incoming, mixed_half[tick_index], CONTRACT_FIRST, preferred_element_type=jnp.float32
        )
    summed = summed_rows(
        jnp.concatenate([sum_project, sum_output], axis=1).astype(jnp.bfloat16), DP, 0
    ).astype(jnp.float32)
    return (summed[None, :, : 3 * head_size], summed[None, :, 3 * head_size :], passed[None])


def solution(mesh):
    split = Mesh(mesh.devices.reshape(mesh.shape["pipe"], 4, 4), ("pipe", "dp_0", "dp_1"))
    in_specs = (
        P("pipe", None, DP, None),
        P("pipe", DP, None),
        P(None, DP, "pipe"),
        P("pipe", DP, None),
        P("pipe", DP, None),
    )
    out_specs = (P("pipe", DP, None), P("pipe", DP, None), P("pipe", DP, None))
    return jax.shard_map(
        shards, mesh=split, in_specs=in_specs, out_specs=out_specs, check_vma=False
    )
```

profile of v0, /device:TPU:1, one launch (start us, length us, event | category | flops | bytes accessed | tf_op | source)
XLA Modules:
  0.0 297.3 jit_solution(1971978237610432667)
XLA Ops:
  7.2 1.8 pad_maximum_fusion.1
  9.0 1.6 broadcast_in_dim.8
  10.6 11.0 %all-to-all-start = ((bf16[32,1,64,128]{3,2,1,0:T(8,128)(2,1)}), bf16[32,1,64,128]{3,2,1,0:T(8,128)(2,1)}, u32[]{:S(2)}, u32[]{:S(2)}) async-start(bf16[32,1,64,128]{3,2,1,0:T(8,128)(2,1)} %broadcast_in_dim.8), calls=%async_computation | async-start | bytes 1048576 | tf_op jit(solution)/shard_map/all_to_all | solution.py:34
  21.7 1.5 convert_reduce_fusion
  23.2 0.1 div.77
  23.3 0.4 multiply_reduce_fusion
  23.7 0.1 rsqrt.43
  23.8 1.4 fusion.7
  25.2 13.4 %all-to-all-done = bf16[32,1,64,128]{3,2,1,0:T(8,128)(2,1)} async-done(((bf16[32,1,64,128]{3,2,1,0:T(8,128)(2,1)}), bf16[32,1,64,128]{3,2,1,0:T(8,128)(2,1)}, u32[]{:S(2)}, u32[]{:S(2)}) %all-to-all-start) | async-done | bytes 524320 | tf_op jit(solution)/shard_map/all_to_all | solution.py:34
  38.6 1.4 copy.11
  40.0 111.5 %all-gather.2.cloned.1.call-done = bf16[4096,512]{1,0:T(8,128)(2,1)} async-done(((bf16[256,512]{1,0:T(8,128)(2,1)}), bf16[4096,512]{1,0:T(8,128)(2,1)}) %all-gather.2.cloned.1.call-update) | async-done | bytes 4194320 | tf_op jit(solution)/shard_map/all_gather | solution.py:19
  151.5 3.1 %fusion.50 = (bf16[128,384]{1,0:T(8,128)(2,1)S(1)}, f32[128,384]{1,0:T(8,128)S(1)}) fusion(bf16[128,4096]{1,0:T(8,128)(2,1)} %get-tuple-element.32, bf16[4096,512]{1,0:T(8,128)(2,1)} %all-gather.2.cloned.1.call-done), kind=kOutput, calls=%fused_computation.116 | convolution fusion | flops 402702336 | bytes 4489216 | tf_op jit(solution)/shard_map/dot_general | solution.py:74
  154.6 0.1 slice_reduce_fusion
  154.7 0.2 multiply_reduce_fusion.3
  155.0 0.1 fusion.43
  155.2 0.2 fusion.49
  155.5 0.3 convolution_convert_fusion.1
  155.8 0.1 multiply_reduce_fusion.10
  156.0 0.3 fusion.40
  156.3 0.2 fusion.41
  156.5 0.1 convolution_convert_fusion.4
  156.6 0.1 multiply_convert_fusion.4
  156.7 0.1 multiply_convert_fusion.3
  156.8 1.2 fusion.37
  158.1 0.3 add_convert_fusion.2
  158.4 3.0 collective-permute-start
  161.4 0.2 convolution_convert_fusion
  161.6 0.5 convolution_bitcast_fusion
  162.1 1.0 fusion.13
  163.1 5.9 %collective-permute-done = bf16[64,4096]{1,0:T(8,128)(2,1)S(1)} collective-permute-done((bf16[64,4096]{1,0:T(8,128)(2,1)S(1)}, bf16[64,4096]{1,0:T(8,128)(2,1)S(1)}, u32[]{:S(2)}, u32[]{:S(2)}) %collective-permute-start) | collective-permute-done | bytes 524320 | tf_op jit(solution)/shard_map/ppermute | solution.py:44
  168.9 0.2 bitcast_select_fusion
  169.2 0.3 convolution_convert_fusion.2
  169.5 0.1 multiply_reduce_fusion.7
  169.7 0.3 fusion.38
  169.9 0.2 fusion.39
  170.2 0.1 convolution_convert_fusion.3
  170.3 0.5 fusion
  170.8 0.1 multiply_convert_fusion.1
  170.9 0.1 multiply_convert_fusion
  171.0 1.0 add_convert_fusion
  172.1 2.2 pad_maximum_fusion
  174.4 49.5 %reduce-scatter.3.cloned.1.call-done = bf16[1024,512]{0,1:T(8,128)(2,1)} async-done(((bf16[4096,512]{0,1:T(8,128)(2,1)}), bf16[1024,512]{0,1:T(8,128)(2,1)}) %reduce-scatter.3.cloned.1.call-update) | async-done | bytes 1048592 | tf_op jit(solution)/shard_map/reduce_scatter | solution.py:49
  223.9 3.1 %fusion.36 = (f32[64]{0:T(128)S(1)}, f32[64]{0:T(128)S(1)}, f32[64,4096]{1,0:T(8,128)S(1)}) fusion(f32[128,4096]{1,0:T(8,128)S(1)} %get-tuple-element.31, bf16[4096,512]{1,0:T(8,128)(2,1)} %all-gather.2.cloned.1.call-done, bf16[64,128]{1,0:T(8,128)(2,1)S(1)} %convolution_convert_fusion.3, bf16[64,128]{1,0:T(8,128)(2,1)S(1)} %multiply_convert_fusion, ...), kind=kOutput, calls=%fused_computation.104 | convolution fusion | flops 202260352 | bytes 5292544 | tf_op jit(solution)/shard_map/dot_general | solution.py:134
  227.0 1.1 fusion.11
  228.1 59.9 %reduce-scatter.5.cloned.1.call-done = bf16[256,512]{0,1:T(8,128)(2,1)} async-done(((bf16[1024,512]{0,1:T(8,128)(2,1)}), bf16[256,512]{0,1:T(8,128)(2,1)}) %reduce-scatter.5.cloned.1.call-update) | async-done | bytes 262160 | tf_op jit(solution)/shard_map/reduce_scatter | solution.py:49
  288.0 1.0 convert_element_type.79
  289.1 0.9 copy.13
  290.0 0.8 copy.14
  (40 shorter events, 0.5 us)
Async XLA Ops:
  7.2 16.1 %copy-start.1 = (bf16[1,2,64,4096]{3,2,1,0:T(8,128)(2,1)S(1)}, bf16[1,2,64,4096]{3,2,1,0:T(8,128)(2,1)}, u32[]{:S(2)}) copy-start(bf16[1,2,64,4096]{3,2,1,0:T(8,128)(2,1)} %param.5) | copy-start | bytes 3145732
  7.2 144.4 %all-gather.2.cloned.1.call-start = ((), (), s32[]{:S(2)}) async-start(), calls=%async_computation.3 | async-start | bytes 4456448 | tf_op jit(solution)/shard_map/all_gather | solution.py:19
  10.6 28.0 %all-to-all-start = ((bf16[32,1,64,128]{3,2,1,0:T(8,128)(2,1)}), bf16[32,1,64,128]{3,2,1,0:T(8,128)(2,1)}, u32[]{:S(2)}, u32[]{:S(2)}) async-start(bf16[32,1,64,128]{3,2,1,0:T(8,128)(2,1)} %broadcast_in_dim.8), calls=%async_computation | async-start | bytes 1048576 | tf_op jit(solution)/shard_map/all_to_all | solution.py:34
  21.7 202.2 %reduce-scatter.3.cloned.1.call-start = ((), (), s32[]{:S(2)}) async-start(), calls=%async_computation.4 | async-start | bytes 5242880 | tf_op jit(solution)/shard_map/reduce_scatter | solution.py:49
  40.0 115.4 %copy-start.3 = (bf16[1,64,4096]{2,1,0:T(8,128)(2,1)S(1)}, bf16[1,64,4096]{2,1,0:T(8,128)(2,1)}, u32[]{:S(2)}) copy-start(bf16[1,64,4096]{2,1,0:T(8,128)(2,1)} %param.6) | copy-start | bytes 1572868
  151.5 3.9 %copy-start = (bf16[4096,512]{1,0:T(8,128)(2,1)S(1)}, bf16[4096,512]{1,0:T(8,128)(2,1)}, u32[]{:S(2)}) copy-start(bf16[4096,512]{1,0:T(8,128)(2,1)} %all-gather.2.cloned.1.call-done) | copy-start | bytes 12582916
  158.1 4.0 %copy-start.2 = (bf16[128,4096]{1,0:T(8,128)(2,1)S(1)}, bf16[128,4096]{1,0:T(8,128)(2,1)}, u32[]{:S(2)}) copy-start(bf16[128,4096]{1,0:T(8,128)(2,1)} %get-tuple-element.32) | copy-start | bytes 3145732
  158.4 10.5 %collective-permute-start = (bf16[64,4096]{1,0:T(8,128)(2,1)S(1)}, bf16[64,4096]{1,0:T(8,128)(2,1)S(1)}, u32[]{:S(2)}, u32[]{:S(2)}) collective-permute-start(bf16[64,4096]{1,0:T(8,128)(2,1)S(1)} %add_convert_fusion.2), channel_id=1, source_target_pairs={{16,0},{32,16},{48,32},{64,48},{80,64},{96,80},{112,96},{128,112},... | collective-permute-start | bytes 1572872 | tf_op jit(solution)/shard_map/ppermute | solution.py:44
  174.3 113.7 %reduce-scatter.5.cloned.1.call-start = ((), (), s32[]{:S(2)}) async-start(), calls=%async_computation.5 | async-start | bytes 1310720 | tf_op jit(solution)/shard_map/reduce_scatter | solution.py:49
Sparse Core Ops, SparseCore 0:
  11.6 139.9 all-gather.1
  174.4 49.3 reduce-scatter.2
  226.7 61.2 reduce-scatter.4
where the time goes:
time: 298 us; the launch traced here: 297 us
  waiting for transfers between devices  240 us (81%)
  starting transfers between devices  14.1 us (5%)
  between operations  14.1 us (5%)
  matrix products  13 us (4%)
  other arithmetic  10.9 us (4%)
  local copies, waits for them, and re-layouts  5.06 us (2%)
    all_gather x1, waiting for transfers between devices, side_by_side(): lax.all_gather(both, axis, axis=dim, tiled=True)  112 us
    reduce_scatter x2, waiting for transfers between devices, summed_rows(): value = lax.psum_scatter(value, axis, scatter_dimension=dim, tiled=True)  109 us
    all_to_all x1, waiting for transfers between devices, copy_for_each(): return lax.all_to_all(copies, axis, split_axis=0, concat_axis=0, tiled=True)  13.4 us
    all_to_all x1, starting transfers between devices, copy_for_each(): return lax.all_to_all(copies, axis, split_axis=0, concat_axis=0, tiled=True)  11 us
  transfers between devices with their start and end apart: 5, of which 5 were waited for; matrix products, arithmetic and copies ran while one was open for 4% of the time, Pallas kernels for 0%

commit v1 on v0

v1 whole, which is shorter than its diff:
```python
import functools
import math

import jax
import jax.numpy as jnp
from jax import lax
from jax.experimental import pallas as pl
from jax.experimental.pallas import tpu as pltpu
from jax.sharding import Mesh
from jax.sharding import PartitionSpec as P

DP = ("dp_0", "dp_1")
MESH = pl.DeviceIdType.MESH
EPSILON = 1e-06
PARTS = 8
ROW_GROUP = 16
CONTRACT_FIRST = (((0,), (0,)), ((), ()))
CONTRACT_LAST = (((1,), (1,)), ((), ()))


def normalize(values):
    centered = values - jnp.mean(values, axis=-1, keepdims=True)
    inverse = lax.rsqrt(jnp.mean(centered * centered, axis=-1, keepdims=True) + EPSILON)
    return (centered * inverse, inverse)


def norm_back(gradient, normed, inverse):
    centered = gradient - jnp.mean(gradient, axis=-1, keepdims=True)
    return inverse * (centered - normed * jnp.mean(gradient * normed, axis=-1, keepdims=True))


def dot32(a, b, dims=None):
    if dims is None:
        return jnp.dot(a, b, preferred_element_type=jnp.float32)
    return lax.dot_general(a, b, dims, preferred_element_type=jnp.float32)


def kernel(
    dims,
    xin,
    arr,
    top,
    wp,
    wo,
    pg_out,
    og_out,
    pass_out,
    xs,
    normed,
    inverse,
    hid,
    hid_t,
    inc,
    inc_t,
    topv,
    full,
    proj_sum,
    head_sum,
    hg,
    sent_back,
    proj_grad,
    mixed,
    part,
    x_relay,
    x_final,
    z_send,
    z_relay,
    z_final,
    own,
    load_sem,
    gather_sem,
    gz_sem,
    gx_sem,
    top_recv,
    top_send,
    pass_recv,
    pass_send,
    xr_sem,
    xf_sem,
    zr_sem,
    zf_sem,
    sx_sem,
    sz_sem,
):
    n_pipe, n_x, n_z, ticks, seq, width, head = dims
    parts, half = PARTS, PARTS // 2
    rows = ticks * seq
    block = width // (n_x * n_z)
    piece = block // parts
    wide = 4 * head
    pw = 3 * head
    root = math.sqrt(head)
    p = lax.axis_index("pipe")
    x = lax.axis_index("dp_0")
    z = lax.axis_index("dp_1")
    x_next, x_prev, x_far = (lax.rem(x + s, n_x) for s in (1, n_x - 1, 2))
    z_next, z_prev, z_far = (lax.rem(z + s, n_z) for s in (1, n_z - 1, 2))
    last = p == n_pipe - 1
    to_x_next, to_x_prev = ({"dp_0": x_next}, {"dp_0": x_prev})
    to_z_next, to_z_prev = ({"dp_1": z_next}, {"dp_1": z_prev})
    pending = []

    def send(src, dst, send_sem, recv_sem, device):
        copy = pltpu.make_async_remote_copy(
            src_ref=src,
            dst_ref=dst,
            send_sem=send_sem,
            recv_sem=recv_sem,
            device_id=device,
            device_id_type=MESH,
        )
        copy.start()
        pending.append(copy)

    def arrived(dst, recv_sem):
        pltpu.make_async_remote_copy(
            src_ref=dst,
            dst_ref=dst,
            send_sem=recv_sem,
            recv_sem=recv_sem,
            device_id=to_x_next,
            device_id_type=MESH,
        ).wait_recv()

    def drain():
        for copy in pending:
            copy.wait_send()
        pending.clear()

    me = x * n_z + z
    loads = [
        pltpu.make_async_copy(xin, xs, load_sem.at[0]),
        pltpu.make_async_copy(wp, full.at[me, :, pl.ds(0, pw)], load_sem.at[1]),
        pltpu.make_async_copy(wo, full.at[me, :, pl.ds(pw, head)], load_sem.at[2]),
        pltpu.make_async_copy(arr, inc.at[pl.ds(0, seq)], load_sem.at[3]),
        pltpu.make_async_copy(top, topv, load_sem.at[4]),
    ]
    for load in loads:
        load.start()

    barrier = pltpu.get_barrier_semaphore()
    for device in (to_x_next, to_x_prev, to_z_next, to_z_prev):
        pl.semaphore_signal(barrier, inc=1, device_id=device, device_id_type=MESH)

    @pl.when(p > 0)
    def _():
        pl.semaphore_signal(barrier, inc=1, device_id={"pipe": p - 1}, device_id_type=MESH)

    @pl.when(p < n_pipe - 1)
    def _():
        pl.semaphore_signal(barrier, inc=1, device_id={"pipe": p + 1}, device_id_type=MESH)
        pl.semaphore_signal(barrier, inc=1, device_id={"pipe": n_pipe - 1}, device_id_type=MESH)

    @pl.when(last)
    def _():
        def greet(i, carry):
            pl.semaphore_signal(barrier, inc=1, device_id={"pipe": i}, device_id_type=MESH)
            return carry

        lax.fori_loop(0, n_pipe - 1, greet, 0)

    loads[0].wait()

    def norm_rows(g, carry):
        at = pl.ds(pl.multiple_of(g * ROW_GROUP, ROW_GROUP), ROW_GROUP)
        values, scale = normalize(xs[at, :].astype(jnp.float32))
        normed[at, :] = values
        hid[at, :] = values.astype(jnp.bfloat16)
        inverse[at, :] = jnp.broadcast_to(scale, (ROW_GROUP, 128))
        return carry

    lax.fori_loop(0, rows // ROW_GROUP, norm_rows, 0)
    for load in loads[1:]:
        load.wait()
    from_neighbours = 4 + jnp.where(p > 0, 1, 0) + jnp.where(last, n_pipe - 1, 2)
    pl.semaphore_wait(barrier, from_neighbours)

    def weight(xx, zz, c):
        return full.at[xx * n_z + zz, pl.ds(c * piece, piece), :]

    def weight_sem(xx, zz, c):
        return gather_sem.at[xx * n_z + zz, c]

    def gather_pair(k):
        phase, j = divmod(k, half)
        za = (z, z_prev, z_next, z_far)[phase]
        zb = (z, z_next, z_prev, z_far)[phase]
        return ((za, j), (zb, half + j))

    def send_weight(xx, at, sem, device):
        zz, c = at
        send(weight(xx, zz, c), weight(xx, zz, c), sem, weight_sem(xx, zz, c), device)

    def weight_arrived(xx, at):
        zz, c = at
        arrived(weight(xx, zz, c), weight_sem(xx, zz, c))

    for j in range(half):
        send_weight(x, (z, j), gz_sem.at[0, j], to_z_next)
        send_weight(x, (z, half + j), gz_sem.at[1, j], to_z_prev)
    for j in range(half):
        send_weight(x, (z, half + j), gz_sem.at[0, half + j], to_z_next)
        send_weight(x, (z, j), gz_sem.at[1, half + j], to_z_prev)

    proj_sum[...] = jnp.zeros_like(proj_sum)
    head_sum[...] = jnp.zeros_like(head_sum)

    def use_block(xx, zz):
        s = xx * n_z + zz
        cols = pl.ds(pl.multiple_of(s * block, block), block)
        proj_sum[...] += dot32(hid[:, cols], full[s, :, :pw])
        head_sum[...] += dot32(inc[:seq, cols], full[s, :, pw:])

    def transpose_block(src, dst, b):
        dst[b * block : (b + 1) * block, :] = src[:, b * block : (b + 1) * block].T

    columns = (x, x_prev, x_next, x_far)
    near = [(xx, z) for xx in columns]
    side = [(xx, zz) for xx in columns for zz in (z_prev, z_next)]
    to_transpose = list(range(n_x * n_z))
    steps = 2 * parts
    for i in range(steps + 3):
        if i < steps:
            a, b = gather_pair(i)
            if i >= half:
                weight_arrived(x, a)
                weight_arrived(x, b)
            if half <= i < parts:
                send_weight(x, a, gz_sem.at[0, i + half], to_z_next)
                send_weight(x, b, gz_sem.at[1, i + half], to_z_prev)
            send_weight(x, a, gx_sem.at[0, i, 0], to_x_next)
            send_weight(x, b, gx_sem.at[1, i, 0], to_x_prev)
            send_weight(x, b, gx_sem.at[0, i, 1], to_x_next)
            send_weight(x, a, gx_sem.at[1, i, 1], to_x_prev)
        if 1 <= i <= steps:
            a, b = gather_pair(i - 1)
            weight_arrived(x_prev, a)
            send_weight(x_prev, a, gx_sem.at[0, i - 1, 2], to_x_next)
            weight_arrived(x_next, b)
            send_weight(x_next, b, gx_sem.at[1, i - 1, 2], to_x_prev)
        if i >= 3:
            a, b = gather_pair(i - 3)
            weight_arrived(x_prev, b)
            weight_arrived(x_next, a)
            weight_arrived(x_far, a)
            weight_arrived(x_far, b)
        if to_transpose:
            transpose_block(hid, hid_t, to_transpose.pop())
        if i > half + 2 and near:
            use_block(*near.pop())
        if i > 3 * half + 2:
            for _ in range(2):
                if side:
                    use_block(*side.pop())
    for b in to_transpose:
        transpose_block(hid, hid_t, b)
    for at in near + side:
        use_block(*at)

    my_cols = pl.ds(pl.multiple_of(p * (width // n_pipe), width // n_pipe), width // n_pipe)
    later = pl.ds(seq, seq)
    top_copy = pltpu.make_async_remote_copy(
        src_ref=topv,
        dst_ref=inc.at[later, my_cols],
        send_sem=top_send,
        recv_sem=top_recv.at[p],
        device_id={"pipe": n_pipe - 1},
        device_id_type=MESH,
    )

    @pl.when(jnp.logical_not(last))
    def _():
        top_copy.start()

    for xx in columns:
        use_block(xx, z_far)

    projected = proj_sum[...]
    query, query_scale = normalize(projected[:, :head])
    key, key_scale = normalize(projected[:, head : 2 * head])
    query_half = query.astype(jnp.bfloat16)
    key_half = key.astype(jnp.bfloat16)
    value_half = projected[:, 2 * head :].astype(jnp.bfloat16)
    attention = []
    for t in range(ticks):
        at = slice(t * seq, (t + 1) * seq)
        powered = jnp.exp(dot32(query_half[at], key_half[at], CONTRACT_LAST) / root)
        attention.append(powered / jnp.sum(powered, axis=-1, keepdims=True))
    attention_half = [a.astype(jnp.bfloat16) for a in attention]

    def head_back(t, head_grad):
        at = slice(t * seq, (t + 1) * seq)
        prob_grad = dot32(head_grad, value_half[at], CONTRACT_LAST)
        value_grad = dot32(attention_half[t], head_grad, CONTRACT_FIRST)
        weighted = attention[t]
        score_grad = (
            weighted
            * (prob_grad - jnp.sum(weighted * prob_grad, axis=-1, keepdims=True))
            / root
        ).astype(jnp.bfloat16)
        query_grad = dot32(score_grad, key_half[at])
        key_grad = dot32(score_grad, query_half[at], CONTRACT_FIRST)
        proj_grad[at, :head] = norm_back(query_grad, query[at], query_scale[at]).astype(
            jnp.bfloat16
        )
        proj_grad[at, head : 2 * head] = norm_back(key_grad, key[at], key_scale[at]).astype(
            jnp.bfloat16
        )
        proj_grad[at, 2 * head :] = value_grad.astype(jnp.bfloat16)

    def hidden_back(t, s):
        hg[:, s * block : (s + 1) * block] = dot32(
            proj_grad[t * seq : (t + 1) * seq, :], full[s, :, :pw], CONTRACT_LAST
        )

    def rows_back(t, g):
        at = slice(g * ROW_GROUP, (g + 1) * ROW_GROUP)
        both = slice(t * seq + g * ROW_GROUP, t * seq + (g + 1) * ROW_GROUP)
        grad = norm_back(hg[at, :], normed[both, :], inverse[both, :1])
        return (inc[both, :].astype(jnp.float32) + grad).astype(jnp.bfloat16)

    head_back(0, head_sum[...].astype(jnp.bfloat16))
    for s in range(n_x * n_z):
        hidden_back(0, s)
    groups = seq // ROW_GROUP
    back_copies = []
    for g in range(groups):
        at = pl.ds(g * ROW_GROUP, ROW_GROUP)
        sent_back[g * ROW_GROUP : (g + 1) * ROW_GROUP, :] = rows_back(0, g)
        back = pltpu.make_async_remote_copy(
            src_ref=sent_back.at[at],
            dst_ref=inc.at[pl.ds(seq + g * ROW_GROUP, ROW_GROUP)],
            send_sem=pass_send.at[g],
            recv_sem=pass_recv.at[g],
            device_id={"pipe": jnp.maximum(p - 1, 0)},
            device_id_type=MESH,
        )
        back_copies.append(back)

        @pl.when(p > 0)
        def _():
            back.start()

    for t in range(ticks):
        at = slice(t * seq, (t + 1) * seq)
        mixed[at, :] = dot32(attention_half[t], value_half[at]).astype(jnp.bfloat16)
    drain()

    @pl.when(last)
    def _():
        top_width = width // n_pipe
        inc[seq:, (n_pipe - 1) * top_width :] = topv[...]

        def one(i, carry):
            cols = pl.ds(pl.multiple_of(i * top_width, top_width), top_width)
            arrived(inc.at[later, cols], top_recv.at[i])
            return carry

        lax.fori_loop(0, n_pipe - 1, one, 0)

    @pl.when(jnp.logical_not(last))
    def _():
        for g in range(groups):
            arrived(inc.at[pl.ds(seq + g * ROW_GROUP, ROW_GROUP)], pass_recv.at[g])

    head_grad = jnp.zeros((seq, head), jnp.float32)
    for s in range(n_x * n_z):
        head_grad += dot32(inc[seq:, s * block : (s + 1) * block], full[s, :, pw:])
        transpose_block(inc, inc_t, s)
    head_back(1, head_grad.astype(jnp.bfloat16))

    def scatter_pair(k):
        phase, j = divmod(k, half)
        za = (z_far, z_prev, z_next, z)[phase]
        zb = (z_far, z_next, z_prev, z)[phase]
        return ((za, j), (zb, half + j))

    around = (x, x_next, x_far, x_prev)
    OWN, NEXT, FAR, PREV = range(4)

    def make_parts(k):
        pieces = []
        for xx in around:
            for zz, c in scatter_pair(k):
                start = (xx * n_z + zz) * block + c * piece
                pieces.append(pl.ds(pl.multiple_of(start, piece), piece))
        projects = dot32(jnp.concatenate([hid_t[at, :] for at in pieces], axis=0), proj_grad[...])
        outputs = dot32(jnp.concatenate([inc_t[at, :] for at in pieces], axis=0), mixed[...])
        for n in range(len(pieces)):
            at = slice(n * piece, (n + 1) * piece)
            part[k, n // 2, n % 2, :, :pw] = projects[at].astype(jnp.bfloat16)
            part[k, n // 2, n % 2, :, pw:] = outputs[at].astype(jnp.bfloat16)

    def added(k, place, ab, relay):
        total = part[k, place, ab].astype(jnp.float32) + relay[...].astype(jnp.float32)
        part[k, place, ab] = total.astype(jnp.bfloat16)

    left, right, hidden_at = 0, 1, 0
    for i in range(steps + 3):
        if i < steps:
            make_parts(i)
            send(part.at[i, FAR, 0], x_relay.at[i, 0], sx_sem.at[i, 0], xr_sem.at[i, 0], to_x_next)
            send(part.at[i, FAR, 1], x_relay.at[i, 1], sx_sem.at[i, 1], xr_sem.at[i, 1], to_x_prev)
            send(
                part.at[i, NEXT, 1],
                x_final.at[i, left, 1],
                sx_sem.at[i, 2],
                xf_sem.at[i, left, 1],
                to_x_next,
            )
            send(
                part.at[i, PREV, 0],
                x_final.at[i, right, 0],
                sx_sem.at[i, 3],
                xf_sem.at[i, right, 0],
                to_x_prev,
            )
        if 1 <= i <= steps:
            k = i - 1
            arrived(x_relay.at[k, 0], xr_sem.at[k, 0])
            added(k, NEXT, 0, x_relay.at[k, 0])
            send(
                part.at[k, NEXT, 0],
                x_final.at[k, left, 0],
                sx_sem.at[k, 4],
                xf_sem.at[k, left, 0],
                to_x_next,
            )
            arrived(x_relay.at[k, 1], xr_sem.at[k, 1])
            added(k, PREV, 1, x_relay.at[k, 1])
            send(
                part.at[k, PREV, 1],
                x_final.at[k, right, 1],
                sx_sem.at[k, 5],
                xf_sem.at[k, right, 1],
                to_x_prev,
            )
        if i >= 3:
            k = i - 3
            phase, j = divmod(k, half)
            for ab in range(2):
                for way in (left, right):
                    arrived(x_final.at[k, way, ab], xf_sem.at[k, way, ab])
                total = (
                    part[k, OWN, ab].astype(jnp.float32)
                    + x_final[k, left, ab].astype(jnp.float32)
                    + x_final[k, right, ab].astype(jnp.float32)
                )
                if phase == 3:
                    own[half * ab + j] = total
                    continue
                if phase == 2:
                    arrived(z_relay.at[j, ab], zr_sem.at[j, ab])
                    total = total + z_relay[j, ab].astype(jnp.float32)
                z_send[k, ab] = total.astype(jnp.bfloat16)
                onward = ab == (1 if phase == 1 else 0)
                device = to_z_next if onward else to_z_prev
                if phase == 0:
                    send(
                        z_send.at[k, ab],
                        z_relay.at[j, ab],
                        sz_sem.at[k, ab],
                        zr_sem.at[j, ab],
                        device,
                    )
                else:
                    way, c = (left if onward else right, half * ab + j)
                    send(
                        z_send.at[k, ab],
                        z_final.at[way, c],
                        sz_sem.at[k, ab],
                        zf_sem.at[way, c],
                        device,
                    )
        if hidden_at < n_x * n_z:
            hidden_back(1, hidden_at)
            hidden_at += 1
    for s in range(hidden_at, n_x * n_z):
        hidden_back(1, s)
    for g in range(groups):
        pass_out[g * ROW_GROUP : (g + 1) * ROW_GROUP, :] = rows_back(1, g)
    for ab in (1, 0):
        for j in range(half):
            c = half * ab + j
            arrived(z_final.at[left, c], zf_sem.at[left, c])
            arrived(z_final.at[right, c], zf_sem.at[right, c])
            total = (
                own[c]
                + z_final[left, c].astype(jnp.float32)
                + z_final[right, c].astype(jnp.float32)
            )
            pg_out[c * piece : (c + 1) * piece, :] = total[:, :pw]
            og_out[c * piece : (c + 1) * piece, :] = total[:, pw:]
    drain()

    @pl.when(p > 0)
    def _():
        for back in back_copies:
            back.wait_send()

    @pl.when(jnp.logical_not(last))
    def _():
        top_copy.wait_send()


def shards(n_pipe, n_x, n_z, section_inputs, arriving, top_grads, project_weights, output_weights):
    _, ticks, seq, width = section_inputs.shape
    head = output_weights.shape[2]
    rows = ticks * seq
    block = width // (n_x * n_z)
    piece = block // PARTS
    half, steps, wide = PARTS // 2, 2 * PARTS, 4 * head
    low, high = jnp.bfloat16, jnp.float32
    dma = pltpu.SemaphoreType.DMA
    scratch = [
        pltpu.VMEM((rows, width), low),
        pltpu.VMEM((rows, width), high),
        pltpu.VMEM((rows, 128), high),
        pltpu.VMEM((rows, width), low),
        pltpu.VMEM((width, rows), low),
        pltpu.VMEM((rows, width), low),
        pltpu.VMEM((width, rows), low),
        pltpu.VMEM((seq, width // n_pipe), low),
        pltpu.VMEM((n_x * n_z, block, wide), low),
        pltpu.VMEM((rows, 3 * head), high),
        pltpu.VMEM((seq, head), high),
        pltpu.VMEM((seq, width), high),
        pltpu.VMEM((seq, width), low),
        pltpu.VMEM((rows, 3 * head), low),
        pltpu.VMEM((rows, head), low),
        pltpu.VMEM((steps, 4, 2, piece, wide), low),
        pltpu.VMEM((steps, 2, piece, wide), low),
        pltpu.VMEM((steps, 2, 2, piece, wide), low),
        pltpu.VMEM((3 * half, 2, piece, wide), low),
        pltpu.VMEM((half, 2, piece, wide), low),
        pltpu.VMEM((2, PARTS, piece, wide), low),
        pltpu.VMEM((PARTS, piece, wide), high),
        dma((5,)),
        dma((n_x * n_z, PARTS)),
        dma((2, 3 * half)),
        dma((2, steps, 3)),
        dma((n_pipe,)),
        dma(()),
        dma((seq // ROW_GROUP,)),
        dma((seq // ROW_GROUP,)),
        dma((steps, 2)),
        dma((steps, 2, 2)),
        dma((half, 2)),
        dma((2, PARTS)),
        dma((steps, 6)),
        dma((3 * half, 2)),
    ]
    anywhere = pl.BlockSpec(memory_space=pl.ANY)
    project, output, passed = pl.pallas_call(
        functools.partial(kernel, (n_pipe, n_x, n_z, ticks, seq, width, head)),
        out_shape=(
            jax.ShapeDtypeStruct((block, 3 * head), high),
            jax.ShapeDtypeStruct((block, head), high),
            jax.ShapeDtypeStruct((seq, width), low),
        ),
        in_specs=[anywhere] * 5,
        out_specs=[pl.BlockSpec(memory_space=pltpu.VMEM)] * 3,
        scratch_shapes=scratch,
        compiler_params=pltpu.CompilerParams(
            collective_id=0, has_side_effects=True, vmem_limit_bytes=60 * 1024 * 1024
        ),
    )(
        section_inputs.reshape(rows, width),
        arriving[0],
        top_grads[0],
        project_weights[0],
        output_weights[0],
    )
    return (project[None], output[None], passed[None])


def solution(mesh):
    n_x = n_z = 4
    split = Mesh(mesh.devices.reshape(mesh.shape["pipe"], n_x, n_z), ("pipe", "dp_0", "dp_1"))
    in_specs = (
        P("pipe", None, DP, None),
        P("pipe", DP, None),
        P(None, DP, "pipe"),
        P("pipe", DP, None),
        P("pipe", DP, None),
    )
    out_specs = (P("pipe", DP, None), P("pipe", DP, None), P("pipe", DP, None))
    return jax.shard_map(
        functools.partial(shards, mesh.shape["pipe"], n_x, n_z),
        mesh=split,
        in_specs=in_specs,
        out_specs=out_specs,
        check_vma=False,
    )
```

time: 298 us -> 123 us (0.41)
  the two profiles are of different devices: /device:TPU:1 before, /device:TPU:97 now
where the time goes in v1:
time: 123 us
  Pallas kernels  119 us (97%)
  local copies, waits for them, and re-layouts  3.29 us (3%)
    pallas_call x1, Pallas kernels, shards(): pl.pallas_call(functools.partial(kernel, (n_pipe, n_x, n_z, ticks, seq, w...  119 us
    unnamed x7, local copies, waits for them, and re-layouts  3.29 us

profile of v1, /device:TPU:97, one launch (start us, length us, event | category | flops | bytes accessed | tf_op | source)
XLA Modules:
  0.0 123.3 jit_solution(10606365584192267537)
XLA Ops:
  0.6 119.3 %shard_map.76 = (f32[256,384]{1,0:T(8,128)}, f32[256,128]{1,0:T(8,128)}, bf16[64,4096]{1,0:T(8,128)(2,1)}) custom-call(bf16[128,4096]{1,0:T(8,128)(2,1)} %bitcast.8, bf16[64,4096]{1,0:T(8,128)(2,1)} %bitcast.9, bf16[64,128]{1,0:T(8,128)(2,1)} %bitcast.15, bf16[256,384]{1,0:T(8,128)(2,1)} %bitcast.12, bf16[256,128]{1,0:T(8,128)(2,1)} %bitcast.14), custom_call_target="tpu_custom_call" | custom-call | tf_op jit(solution)/shard_map/pallas_call | solution.py:554
  120.0 0.0 copy-start.1
  120.0 0.0 copy-start
  120.0 1.8 %copy.11 = f32[1,256,384]{2,1,0:T(8,128)} copy(f32[1,256,384]{2,1,0:T(8,128)} %bitcast.11) | data formatting | bytes 786432
  121.8 0.0 copy-done.1
  121.8 0.7 copy.12
  122.5 0.0 copy-done
  122.5 0.8 copy.13
Async XLA Ops:
  120.0 1.9 %copy-start.1 = (f32[256,128]{1,0:T(8,128)S(1)}, f32[256,128]{1,0:T(8,128)}, u32[]{:S(2)}) copy-start(f32[256,128]{1,0:T(8,128)} %get-tuple-element.7) | copy-start | bytes 393220
  120.0 2.5 %copy-start = (bf16[64,4096]{1,0:T(8,128)(2,1)S(1)}, bf16[64,4096]{1,0:T(8,128)(2,1)}, u32[]{:S(2)}) copy-start(bf16[64,4096]{1,0:T(8,128)(2,1)} %get-tuple-element.8) | copy-start | bytes 1572868

commit v2 on v1

--- a/solution.py
+++ b/solution.py
@@ -13,6 +13,7 @@
 MESH = pl.DeviceIdType.MESH
 EPSILON = 1e-06
 PARTS = 8
+SLOW_WINDOW = 2
 ROW_GROUP = 16
 CONTRACT_FIRST = (((0,), (0,)), ((), ()))
 CONTRACT_LAST = (((1,), (1,)), ((), ()))
@@ -100,7 +101,7 @@
     to_z_next, to_z_prev = ({"dp_1": z_next}, {"dp_1": z_prev})
     pending = []
 
-    def send(src, dst, send_sem, recv_sem, device):
+    def send(src, dst, send_sem, recv_sem, device, keep=True):
         copy = pltpu.make_async_remote_copy(
             src_ref=src,
             dst_ref=dst,
@@ -110,7 +111,8 @@
             device_id_type=MESH,
         )
         copy.start()
-        pending.append(copy)
+        if keep:
+            pending.append(copy)
 
     def arrived(dst, recv_sem):
         pltpu.make_async_remote_copy(
@@ -122,6 +124,16 @@
             device_id_type=MESH,
         ).wait_recv()
 
+    def sent(src, send_sem):
+        pltpu.make_async_remote_copy(
+            src_ref=src,
+            dst_ref=src,
+            send_sem=send_sem,
+            recv_sem=send_sem,
+            device_id=to_x_next,
+            device_id_type=MESH,
+        ).wait_send()
+
     def drain():
         for copy in pending:
             copy.wait_send()
@@ -129,9 +141,9 @@
 
     me = x * n_z + z
     loads = [
-        pltpu.make_async_copy(xin, xs, load_sem.at[0]),
-        pltpu.make_async_copy(wp, full.at[me, :, pl.ds(0, pw)], load_sem.at[1]),
-        pltpu.make_async_copy(wo, full.at[me, :, pl.ds(pw, head)], load_sem.at[2]),
+        pltpu.make_async_copy(wp, full.at[me, :, pl.ds(0, pw)], load_sem.at[0]),
+        pltpu.make_async_copy(wo, full.at[me, :, pl.ds(pw, head)], load_sem.at[1]),
+        pltpu.make_async_copy(xin, xs, load_sem.at[2]),
         pltpu.make_async_copy(arr, inc.at[pl.ds(0, seq)], load_sem.at[3]),
         pltpu.make_async_copy(top, topv, load_sem.at[4]),
     ]
@@ -160,6 +172,67 @@
         lax.fori_loop(0, n_pipe - 1, greet, 0)
 
     loads[0].wait()
+    loads[1].wait()
+    from_neighbours = 4 + jnp.where(p > 0, 1, 0) + jnp.where(last, n_pipe - 1, 2)
+    pl.semaphore_wait(barrier, from_neighbours)
+
+    def weight(xx, zz, c):
+        return full.at[xx * n_z + zz, pl.ds(c * piece, piece), :]
+
+    def weight_sem(xx, zz, c):
+        return gather_sem.at[xx * n_z + zz, c]
+
+    def gather_pair(k):
+        phase, j = divmod(k, half)
+        za = (z, z_prev, z_next, z_far)[phase]
+        zb = (z, z_next, z_prev, z_far)[phase]
+        return ((za, j), (zb, half + j))
+
+    def send_weight(xx, at, sem, device, keep=True):
+        zz, c = at
+        send(weight(xx, zz, c), weight(xx, zz, c), sem, weight_sem(xx, zz, c), device, keep)
+
+    def weight_arrived(xx, at):
+        zz, c = at
+        arrived(weight(xx, zz, c), weight_sem(xx, zz, c))
+
+    ahead = lax.rem(p, 2) == 0
+    n_items = parts + half
+
+    def z_item(n):
+        if n < half:
+            up, down = (z, n), (z, half + n)
+        elif n < parts:
+            up, down = (z, n), (z, n - half)
+        else:
+            up, down = gather_pair(half + n - parts)
+        send_weight(x, up, gz_sem.at[0, n], to_z_next, False)
+        send_weight(x, down, gz_sem.at[1, n], to_z_prev, False)
+
+    def z_items(first, slow_first, count, slow_count):
+        @pl.when(ahead)
+        def _():
+            for n in range(first, min(first + count, n_items)):
+                z_item(n)
+
+        @pl.when(jnp.logical_not(ahead))
+        def _():
+            for n in range(slow_first, min(slow_first + slow_count, n_items)):
+                z_item(n)
+
+    z_items(0, 0, parts, SLOW_WINDOW)
+
+    def share_pair(i):
+        a, b = gather_pair(i)
+        send_weight(x, a, gx_sem.at[0, i, 0], to_x_next)
+        send_weight(x, b, gx_sem.at[1, i, 0], to_x_prev)
+        send_weight(x, b, gx_sem.at[0, i, 1], to_x_next)
+        send_weight(x, a, gx_sem.at[1, i, 1], to_x_prev)
+
+    for i in range(half):
+        share_pair(i)
+
+    loads[2].wait()
 
     def norm_rows(g, carry):
         at = pl.ds(pl.multiple_of(g * ROW_GROUP, ROW_GROUP), ROW_GROUP)
@@ -170,54 +243,26 @@
         return carry
 
     lax.fori_loop(0, rows // ROW_GROUP, norm_rows, 0)
-    for load in loads[1:]:
+    for load in loads[3:]:
         load.wait()
-    from_neighbours = 4 + jnp.where(p > 0, 1, 0) + jnp.where(last, n_pipe - 1, 2)
-    pl.semaphore_wait(barrier, from_neighbours)
-
-    def weight(xx, zz, c):
-        return full.at[xx * n_z + zz, pl.ds(c * piece, piece), :]
-
-    def weight_sem(xx, zz, c):
-        return gather_sem.at[xx * n_z + zz, c]
-
-    def gather_pair(k):
-        phase, j = divmod(k, half)
-        za = (z, z_prev, z_next, z_far)[phase]
-        zb = (z, z_next, z_prev, z_far)[phase]
-        return ((za, j), (zb, half + j))
-
-    def send_weight(xx, at, sem, device):
-        zz, c = at
-        send(weight(xx, zz, c), weight(xx, zz, c), sem, weight_sem(xx, zz, c), device)
-
-    def weight_arrived(xx, at):
-        zz, c = at
-        arrived(weight(xx, zz, c), weight_sem(xx, zz, c))
-
-    for j in range(half):
-        send_weight(x, (z, j), gz_sem.at[0, j], to_z_next)
-        send_weight(x, (z, half + j), gz_sem.at[1, j], to_z_prev)
-    for j in range(half):
-        send_weight(x, (z, half + j), gz_sem.at[0, half + j], to_z_next)
-        send_weight(x, (z, j), gz_sem.at[1, half + j], to_z_prev)
 
     proj_sum[...] = jnp.zeros_like(proj_sum)
     head_sum[...] = jnp.zeros_like(head_sum)
 
-    def use_block(xx, zz):
-        s = xx * n_z + zz
-        cols = pl.ds(pl.multiple_of(s * block, block), block)
-        proj_sum[...] += dot32(hid[:, cols], full[s, :, :pw])
-        head_sum[...] += dot32(inc[:seq, cols], full[s, :, pw:])
+    def use_blocks(places):
+        project, output = 0.0, 0.0
+        for xx, zz in places:
+            s = xx * n_z + zz
+            cols = pl.ds(pl.multiple_of(s * block, block), block)
+            project += dot32(hid[:, cols], full[s, :, :pw])
+            output += dot32(inc[:seq, cols], full[s, :, pw:])
+        proj_sum[...] += project
+        head_sum[...] += output
 
     def transpose_block(src, dst, b):
         dst[b * block : (b + 1) * block, :] = src[:, b * block : (b + 1) * block].T
 
     columns = (x, x_prev, x_next, x_far)
-    near = [(xx, z) for xx in columns]
-    side = [(xx, zz) for xx in columns for zz in (z_prev, z_next)]
-    to_transpose = list(range(n_x * n_z))
     steps = 2 * parts
     for i in range(steps + 3):
         if i < steps:
@@ -225,13 +270,8 @@
             if i >= half:
                 weight_arrived(x, a)
                 weight_arrived(x, b)
-            if half <= i < parts:
-                send_weight(x, a, gz_sem.at[0, i + half], to_z_next)
-                send_weight(x, b, gz_sem.at[1, i + half], to_z_prev)
-            send_weight(x, a, gx_sem.at[0, i, 0], to_x_next)
-            send_weight(x, b, gx_sem.at[1, i, 0], to_x_prev)
-            send_weight(x, b, gx_sem.at[0, i, 1], to_x_next)
-            send_weight(x, a, gx_sem.at[1, i, 1], to_x_prev)
+                z_items(parts + i - half, SLOW_WINDOW + i - half, 1, 1)
+                share_pair(i)
         if 1 <= i <= steps:
             a, b = gather_pair(i - 1)
             weight_arrived(x_prev, a)
@@ -244,18 +284,15 @@
             weight_arrived(x_next, a)
             weight_arrived(x_far, a)
             weight_arrived(x_far, b)
-        if to_transpose:
-            transpose_block(hid, hid_t, to_transpose.pop())
-        if i > half + 2 and near:
-            use_block(*near.pop())
-        if i > 3 * half + 2:
-            for _ in range(2):
-                if side:
-                    use_block(*side.pop())
-    for b in to_transpose:
-        transpose_block(hid, hid_t, b)
-    for at in near + side:
-        use_block(*at)
+        if 1 <= i <= parts:
+            for b in range(2 * i - 2, 2 * i):
+                transpose_block(hid, hid_t, b)
+        if i == half + 2:
+            use_blocks([(xx, z) for xx in columns])
+        if i == 3 * half + 2:
+            use_blocks([(xx, zz) for xx in columns for zz in (z_prev, z_next)])
+        if i == steps:
+            use_blocks([(x, z_far)])
 
     my_cols = pl.ds(pl.multiple_of(p * (width // n_pipe), width // n_pipe), width // n_pipe)
     later = pl.ds(seq, seq)
@@ -272,8 +309,7 @@
     def _():
         top_copy.start()
 
-    for xx in columns:
-        use_block(xx, z_far)
+    use_blocks([(xx, z_far) for xx in (x_prev, x_next, x_far)])
 
     projected = proj_sum[...]
     query, query_scale = normalize(projected[:, :head])
@@ -345,6 +381,9 @@
         at = slice(t * seq, (t + 1) * seq)
         mixed[at, :] = dot32(attention_half[t], value_half[at]).astype(jnp.bfloat16)
     drain()
+    for n in range(n_items):
+        for way in range(2):
+            sent(weight(x, z, 0), gz_sem.at[way, n])
 
     @pl.when(last)
     def _():
@@ -503,6 +542,15 @@
         top_copy.wait_send()
 
 
+def put_out(pg_in, og_in, pass_in, pg_out, og_out, pass_out, sems):
+    pairs = ((pg_in, pg_out), (og_in, og_out), (pass_in, pass_out))
+    copies = [pltpu.make_async_copy(a, b, sems.at[n]) for n, (a, b) in enumerate(pairs)]
+    for copy in copies:
+        copy.start()
+    for copy in copies:
+        copy.wait()
+
+
 def shards(n_pipe, n_x, n_z, section_inputs, arriving, top_grads, project_weights, output_weights):
     _, ticks, seq, width = section_inputs.shape
     head = output_weights.shape[2]
@@ -551,18 +599,18 @@
         dma((3 * half, 2)),
     ]
     anywhere = pl.BlockSpec(memory_space=pl.ANY)
-    project, output, passed = pl.pallas_call(
+    results = pl.pallas_call(
         functools.partial(kernel, (n_pipe, n_x, n_z, ticks, seq, width, head)),
         out_shape=(
-            jax.ShapeDtypeStruct((block, 3 * head), high),
-            jax.ShapeDtypeStruct((block, head), high),
-            jax.ShapeDtypeStruct((seq, width), low),
+            pltpu.VMEM((block, 3 * head), high),
+            pltpu.VMEM((block, head), high),
+            pltpu.VMEM((seq, width), low),
         ),
-        in_specs=[anywhere] * 5,
+        in_specs=[pl.BlockSpec(memory_space=pltpu.HBM)] * 5,
         out_specs=[pl.BlockSpec(memory_space=pltpu.VMEM)] * 3,
         scratch_shapes=scratch,
         compiler_params=pltpu.CompilerParams(
-            collective_id=0, has_side_effects=True, vmem_limit_bytes=60 * 1024 * 1024
+            collective_id=0, has_side_effects=True, vmem_limit_bytes=65_900_000
         ),
     )(
         section_inputs.reshape(rows, width),
@@ -571,6 +619,18 @@
         project_weights[0],
         output_weights[0],
     )
+    project, output, passed = pl.pallas_call(
+        put_out,
+        out_shape=(
+            jax.ShapeDtypeStruct((block, 3 * head), high),
+            jax.ShapeDtypeStruct((block, head), high),
+            jax.ShapeDtypeStruct((seq, width), low),
+        ),
+        in_specs=[pl.BlockSpec(memory_space=pltpu.VMEM)] * 3,
+        out_specs=[anywhere] * 3,
+        scratch_shapes=[dma((3,))],
+        compiler_params=pltpu.CompilerParams(vmem_limit_bytes=4 * 1024 * 1024),
+    )(*results)
     return (project[None], output[None], passed[None])
 
 

time: 123 us -> 117 us (0.951)
  the two profiles are of different devices: /device:TPU:97 before, /device:TPU:16 now
where the time goes in v2:
time: 117 us
  Pallas kernels  117 us (100%)
    pallas_call x1, Pallas kernels, shards(): pl.pallas_call(functools.partial(kernel, (n_pipe, n_x, n_z, ticks, seq, w...  116 us

profile of v2, /device:TPU:16, one launch (start us, length us, event | category | flops | bytes accessed | tf_op | source)
XLA Modules:
  0.0 117.3 jit_solution(15890293946779107096)
XLA Ops:
  0.6 115.7 %shard_map.76 = (f32[256,384]{1,0:T(8,128)S(1)}, f32[256,128]{1,0:T(8,128)S(1)}, bf16[64,4096]{1,0:T(8,128)(2,1)S(1)}) custom-call(bf16[128,4096]{1,0:T(8,128)(2,1)} %bitcast.8, bf16[64,4096]{1,0:T(8,128)(2,1)} %bitcast.9, bf16[64,128]{1,0:T(8,128)(2,1)} %bitcast.12, bf16[256,384]{1,0:T(8,128)(2,1)} %bitcast.10, bf16[256,128]{1,0:T(8,128)(2,1)} %bitcast.11), custom_call_target="tpu_custom_call" | custom-call | tf_op jit(solution)/shard_map/pallas_call | solution.py:602
  116.3 1.0 shard_map.77

commit v3 on v2

--- a/solution.py
+++ b/solution.py
@@ -82,6 +82,7 @@
     zf_sem,
     sx_sem,
     sz_sem,
+    top_ready,
 ):
     n_pipe, n_x, n_z, ticks, seq, width, head = dims
     parts, half = PARTS, PARTS // 2
@@ -163,17 +164,9 @@
         pl.semaphore_signal(barrier, inc=1, device_id={"pipe": p + 1}, device_id_type=MESH)
         pl.semaphore_signal(barrier, inc=1, device_id={"pipe": n_pipe - 1}, device_id_type=MESH)
 
-    @pl.when(last)
-    def _():
-        def greet(i, carry):
-            pl.semaphore_signal(barrier, inc=1, device_id={"pipe": i}, device_id_type=MESH)
-            return carry
-
-        lax.fori_loop(0, n_pipe - 1, greet, 0)
-
     loads[0].wait()
     loads[1].wait()
-    from_neighbours = 4 + jnp.where(p > 0, 1, 0) + jnp.where(last, n_pipe - 1, 2)
+    from_neighbours = 4 + jnp.where(p > 0, 1, 0) + jnp.where(last, n_pipe - 1, 1)
     pl.semaphore_wait(barrier, from_neighbours)
 
     def weight(xx, zz, c):
@@ -245,6 +238,14 @@
     lax.fori_loop(0, rows // ROW_GROUP, norm_rows, 0)
     for load in loads[3:]:
         load.wait()
+
+    @pl.when(last)
+    def _():
+        def ready(i, carry):
+            pl.semaphore_signal(top_ready, inc=1, device_id={"pipe": i}, device_id_type=MESH)
+            return carry
+
+        lax.fori_loop(0, n_pipe - 1, ready, 0)
 
     proj_sum[...] = jnp.zeros_like(proj_sum)
     head_sum[...] = jnp.zeros_like(head_sum)
@@ -307,6 +308,7 @@
 
     @pl.when(jnp.logical_not(last))
     def _():
+        pl.semaphore_wait(top_ready, 1)
         top_copy.start()
 
     use_blocks([(xx, z_far) for xx in (x_prev, x_next, x_far)])
@@ -597,6 +599,7 @@
         dma((2, PARTS)),
         dma((steps, 6)),
         dma((3 * half, 2)),
+        pltpu.SemaphoreType.REGULAR,
     ]
     anywhere = pl.BlockSpec(memory_space=pl.ANY)
     results = pl.pallas_call(

time: 117 us -> 118 us (level)
  no operation moved by 1% of the time
where the time goes in v3:
time: 118 us
  Pallas kernels  117 us (99%)
    pallas_call x1, Pallas kernels, shards(): pl.pallas_call(functools.partial(kernel, (n_pipe, n_x, n_z, ticks, seq, w...  116 us

profile of v3, /device:TPU:16, one launch (start us, length us, event | category | flops | bytes accessed | tf_op | source)
XLA Modules:
  0.0 117.6 jit_solution(6968728743380477224)
XLA Ops:
  0.6 116.0 %shard_map.76 = (f32[256,384]{1,0:T(8,128)S(1)}, f32[256,128]{1,0:T(8,128)S(1)}, bf16[64,4096]{1,0:T(8,128)(2,1)S(1)}) custom-call(bf16[128,4096]{1,0:T(8,128)(2,1)} %bitcast.8, bf16[64,4096]{1,0:T(8,128)(2,1)} %bitcast.9, bf16[64,128]{1,0:T(8,128)(2,1)} %bitcast.12, bf16[256,384]{1,0:T(8,128)(2,1)} %bitcast.10, bf16[256,128]{1,0:T(8,128)(2,1)} %bitcast.11), custom_call_target="tpu_custom_call" | custom-call | tf_op jit(solution)/shard_map/pallas_call | solution.py:605
  116.6 1.0 shard_map.77

commit v4 on v3

--- a/solution.py
+++ b/solution.py
@@ -13,7 +13,7 @@
 MESH = pl.DeviceIdType.MESH
 EPSILON = 1e-06
 PARTS = 8
-SLOW_WINDOW = 2
+WINDOWS = ((8, 2), (4, 3), (4, 3), (4, 2))
 ROW_GROUP = 16
 CONTRACT_FIRST = (((0,), (0,)), ((), ()))
 CONTRACT_LAST = (((1,), (1,)), ((), ()))
@@ -189,7 +189,13 @@
         zz, c = at
         arrived(weight(xx, zz, c), weight_sem(xx, zz, c))
 
-    ahead = lax.rem(p, 2) == 0
+    place = lax.rem(p // 2, len(WINDOWS))
+    window_of = {}
+    for spot, windows in enumerate(WINDOWS):
+        for core, window in enumerate(windows):
+            here = jnp.logical_and(place == spot, lax.rem(p, 2) == core)
+            known = window_of.get(window)
+            window_of[window] = here if known is None else jnp.logical_or(known, here)
     n_items = parts + half
 
     def z_item(n):
@@ -202,18 +208,15 @@
         send_weight(x, up, gz_sem.at[0, n], to_z_next, False)
         send_weight(x, down, gz_sem.at[1, n], to_z_prev, False)
 
-    def z_items(first, slow_first, count, slow_count):
-        @pl.when(ahead)
-        def _():
-            for n in range(first, min(first + count, n_items)):
-                z_item(n)
-
-        @pl.when(jnp.logical_not(ahead))
-        def _():
-            for n in range(slow_first, min(slow_first + slow_count, n_items)):
-                z_item(n)
-
-    z_items(0, 0, parts, SLOW_WINDOW)
+    def z_items(first, stop):
+        for window, here in window_of.items():
+
+            @pl.when(here)
+            def _():
+                for n in range(max(window + first, 0), min(window + stop, n_items)):
+                    z_item(n)
+
+    z_items(-n_items, 0)
 
     def share_pair(i):
         a, b = gather_pair(i)
@@ -271,7 +274,7 @@
             if i >= half:
                 weight_arrived(x, a)
                 weight_arrived(x, b)
-                z_items(parts + i - half, SLOW_WINDOW + i - half, 1, 1)
+                z_items(i - half, i - half + 1)
                 share_pair(i)
         if 1 <= i <= steps:
             a, b = gather_pair(i - 1)
@@ -437,6 +440,44 @@
         part[k, place, ab] = total.astype(jnp.bfloat16)
 
     left, right, hidden_at = 0, 1, 0
+
+    def finish(k):
+        phase, j = divmod(k, half)
+        for ab in range(2):
+            for way in (left, right):
+                arrived(x_final.at[k, way, ab], xf_sem.at[k, way, ab])
+            total = (
+                part[k, OWN, ab].astype(jnp.float32)
+                + x_final[k, left, ab].astype(jnp.float32)
+                + x_final[k, right, ab].astype(jnp.float32)
+            )
+            if phase == 3:
+                own[half * ab + j] = total
+                continue
+            if phase == 2:
+                arrived(z_relay.at[j, ab], zr_sem.at[j, ab])
+                total = total + z_relay[j, ab].astype(jnp.float32)
+            z_send[k, ab] = total.astype(jnp.bfloat16)
+            onward = ab == (1 if phase == 1 else 0)
+            device = to_z_next if onward else to_z_prev
+            if phase == 0:
+                send(
+                    z_send.at[k, ab],
+                    z_relay.at[j, ab],
+                    sz_sem.at[k, ab],
+                    zr_sem.at[j, ab],
+                    device,
+                )
+            else:
+                way, c = (left if onward else right, half * ab + j)
+                send(
+                    z_send.at[k, ab],
+                    z_final.at[way, c],
+                    sz_sem.at[k, ab],
+                    zf_sem.at[way, c],
+                    device,
+                )
+
     for i in range(steps + 3):
         if i < steps:
             make_parts(i)
@@ -477,42 +518,7 @@
                 to_x_prev,
             )
         if i >= 3:
-            k = i - 3
-            phase, j = divmod(k, half)
-            for ab in range(2):
-                for way in (left, right):
-                    arrived(x_final.at[k, way, ab], xf_sem.at[k, way, ab])
-                total = (
-                    part[k, OWN, ab].astype(jnp.float32)
-                    + x_final[k, left, ab].astype(jnp.float32)
-                    + x_final[k, right, ab].astype(jnp.float32)
-                )
-                if phase == 3:
-                    own[half * ab + j] = total
-                    continue
-                if phase == 2:
-                    arrived(z_relay.at[j, ab], zr_sem.at[j, ab])
-                    total = total + z_relay[j, ab].astype(jnp.float32)
-                z_send[k, ab] = total.astype(jnp.bfloat16)
-                onward = ab == (1 if phase == 1 else 0)
-                device = to_z_next if onward else to_z_prev
-                if phase == 0:
-                    send(
-                        z_send.at[k, ab],
-                        z_relay.at[j, ab],
-                        sz_sem.at[k, ab],
-                        zr_sem.at[j, ab],
-                        device,
-                    )
-                else:
-                    way, c = (left if onward else right, half * ab + j)
-                    send(
-                        z_send.at[k, ab],
-                        z_final.at[way, c],
-                        sz_sem.at[k, ab],
-                        zf_sem.at[way, c],
-                        device,
-                    )
+            finish(i - 3)
         if hidden_at < n_x * n_z:
             hidden_back(1, hidden_at)
             hidden_at += 1

time: 118 us -> 116 us (0.983)
  the two profiles are of different devices: /device:TPU:16 before, /device:TPU:22 now
where the time goes in v4:
time: 116 us
  Pallas kernels  115 us (99%)
    pallas_call x1, Pallas kernels, shards(): pl.pallas_call(functools.partial(kernel, (n_pipe, n_x, n_z, ticks, seq, w...  114 us

profile of v4, /device:TPU:22, one launch (start us, length us, event | category | flops | bytes accessed | tf_op | source)
XLA Modules:
  0.0 115.9 jit_solution(6205737377610588018)
XLA Ops:
  0.6 114.3 %shard_map.76 = (f32[256,384]{1,0:T(8,128)S(1)}, f32[256,128]{1,0:T(8,128)S(1)}, bf16[64,4096]{1,0:T(8,128)(2,1)S(1)}) custom-call(bf16[128,4096]{1,0:T(8,128)(2,1)} %bitcast.8, bf16[64,4096]{1,0:T(8,128)(2,1)} %bitcast.9, bf16[64,128]{1,0:T(8,128)(2,1)} %bitcast.12, bf16[256,384]{1,0:T(8,128)(2,1)} %bitcast.10, bf16[256,128]{1,0:T(8,128)(2,1)} %bitcast.11), custom_call_target="tpu_custom_call" | custom-call | tf_op jit(solution)/shard_map/pallas_call | solution.py:611
  114.9 1.0 shard_map.77
